TPU v7x, 32 devices: a whole 2x2x4 slice. The times are simulated.
32 devices in a mesh: cplx: 4 (over y, core), dap: 8 (over z, x).
Axes of the slice: x: 2, y: 2, z: 4, core: 2. Of those that a mesh axis runs over, the one named last changes fastest.
Arguments:
- alignment_features: bfloat16 [64, 64, 256], P(('cplx', 'dap')), parts along dimension 0, may hold values from -6 to 6
- couple_features: bfloat16 [256, 64, 128], P(('cplx', 'dap')), parts along dimension 0, may hold values from -6 to 6
- alignment_presence: int32 [64, 64], P('cplx'), parts along dimension 0, may hold values 0 or 1
- amino_presence: int32 [256], P('cplx'), parts along dimension 0, may hold values 0 or 1
- strand_identity: int32 [256], P('cplx'), parts along dimension 0, may hold values from 0 to 3, never falling along the last dimension, each value on 1 to 32 neighbouring positions
- strand_couple_embedding: float32 [2, 128], replicated, may hold values from -4 to 4
- fourfold_input_matrix: bfloat16 [256, 1024], replicated, may hold values from -0.375 to 0.375
- heads_merge_matrix: bfloat16 [256, 256], replicated, may hold values from -1.5 to 1.5
- couple_logit_matrix: bfloat16 [128, 8], replicated, may hold values from -30 to 30
- twin_factor_matrix: bfloat16 [256, 64], replicated, may hold values from -0.375 to 0.375
- tensor_reduce_matrix: bfloat16 [1024, 128], replicated, may hold values from -0.75 to 0.75
Outputs:
- alignment_mixed: bfloat16 [64, 64, 256], P(('cplx', 'dap')), parts along dimension 0
- couple_refreshed: bfloat16 [256, 64, 128], P(('cplx', 'dap')), parts along dimension 0
There are 4 independent parts, one for each index of `cplx`. A program takes and returns all parts, laid end to end along the dimension named above; an argument that names none is the same for every part. Nothing has to cross between parts.
All inputs are finite; a program needn't handle non-finite values.
Results may differ from a plain program's by a relative error of at most 0.0075.
The roundings to bfloat16 on the way count: a program that leaves them out, or rounds other values in their place, can miss the bound.
Values may be sent and summed in bfloat16 or wider, within the bound.
No kernel may reach another device: no remote copies, remote signals or barrier semaphores. Data moves between devices by JAX's collectives and lax.ppermute only.
A program may use at most 64 MiB of HBM per device.

v0:
```python
import jax
import jax.numpy as jnp
from jax import lax
from jax.sharding import PartitionSpec as P

EPS = 1e-05


def standardize_features(x):
    x = x.astype(jnp.float32)
    center = x - jnp.mean(x, axis=-1, keepdims=True)
    spread = jnp.mean(center * center, axis=-1, keepdims=True)
    return center * lax.rsqrt(spread + EPS)


def on_device(
    alignment_features,
    couple_features,
    alignment_presence,
    amino_presence,
    strand_identity,
    strand_couple_embedding,
    fourfold_input_matrix,
    heads_merge_matrix,
    couple_logit_matrix,
    twin_factor_matrix,
    tensor_reduce_matrix,
):
    res_here = couple_features.shape[0]
    every_amino_line = couple_features.shape[1]
    device_aligned_lines = alignment_features.shape[0]
    width = twin_factor_matrix.shape[1] // 2
    head_count = couple_logit_matrix.shape[1]
    head_size = heads_merge_matrix.shape[0] // head_count
    position = lax.axis_index("dap")
    res_start = position * res_here
    seq_start = position * device_aligned_lines
    chain_here = lax.dynamic_slice_in_dim(strand_identity, res_start, res_here)
    same = (chain_here[:, None] == strand_identity[None, :]).astype(jnp.float32)[..., None]
    z_in = (
        couple_features.astype(jnp.float32)
        + (1.0 - same) * strand_couple_embedding[0]
        + same * strand_couple_embedding[1]
    )
    pair_ln = standardize_features(z_in).astype(jnp.bfloat16)
    bias_here = jnp.einsum(
        "ijc,ch->hij", pair_ln, couple_logit_matrix, preferred_element_type=jnp.float32
    ).astype(jnp.bfloat16)
    bias_all = lax.all_gather(bias_here, "dap", axis=1, tiled=True)
    presence_numeric = alignment_presence.astype(jnp.float32)
    mask_rows = lax.dynamic_slice_in_dim(presence_numeric, seq_start, device_aligned_lines, 0)
    standardized_alignment = standardize_features(alignment_features).astype(jnp.bfloat16)
    mapped_lines = jnp.dot(
        standardized_alignment.reshape(
            device_aligned_lines * every_amino_line, alignment_features.shape[2]
        ),
        fourfold_input_matrix,
        preferred_element_type=jnp.float32,
    )
    mapped_lines = mapped_lines.reshape(
        device_aligned_lines, every_amino_line, 4, head_count, head_size
    )
    asking_vectors = (mapped_lines[:, :, 0] * head_size ** (-0.5)).astype(jnp.bfloat16)
    target_vectors = mapped_lines[:, :, 1].astype(jnp.bfloat16)
    content_vectors = mapped_lines[:, :, 2].astype(jnp.bfloat16)
    sigmoid_factors = jax.nn.sigmoid(mapped_lines[:, :, 3])
    scores = jnp.einsum(
        "sihd,sjhd->shij", asking_vectors, target_vectors, preferred_element_type=jnp.float32
    )
    scores = (
        scores
        + bias_all.astype(jnp.float32)[None]
        + ((mask_rows - 1.0) * 1000000000.0)[:, None, None, :]
    )
    weights = jax.nn.softmax(scores, axis=-1).astype(jnp.bfloat16)
    context = jnp.einsum(
        "shij,sjhd->sihd", weights, content_vectors, preferred_element_type=jnp.float32
    )
    gated_values = (
        (sigmoid_factors * context)
        .astype(jnp.bfloat16)
        .reshape(device_aligned_lines * every_amino_line, head_count * head_size)
    )
    offset_lines = jnp.dot(
        gated_values, heads_merge_matrix, preferred_element_type=jnp.float32
    ).reshape(alignment_features.shape)
    alignment_mixed = (alignment_features.astype(jnp.float32) + offset_lines).astype(jnp.bfloat16)
    mask_cols = lax.dynamic_slice_in_dim(presence_numeric, res_start, res_here, 1)
    count = jnp.dot(mask_cols.T, presence_numeric, precision=lax.Precision.HIGHEST) + 1.0
    rows_ln = standardize_features(alignment_mixed).astype(jnp.bfloat16)
    twin_factor_features = jnp.einsum(
        "sjm,mk->jsk", rows_ln, twin_factor_matrix, preferred_element_type=jnp.float32
    )
    mask_t = mask_rows.T[..., None]
    left_rows = (
        (twin_factor_features[:, :, :width] * mask_t)
        .astype(jnp.bfloat16)
        .reshape(every_amino_line, device_aligned_lines * width)
    )
    right_rows = (
        (twin_factor_features[:, :, width:] * mask_t)
        .astype(jnp.bfloat16)
        .reshape(every_amino_line, device_aligned_lines * width)
    )
    left_full = lax.all_to_all(left_rows, "dap", split_axis=0, concat_axis=1, tiled=True)
    piece = lax.all_gather(right_rows, "dap", axis=1, tiled=True)
    columns = piece.shape[1]
    left_part = left_full.reshape(res_here, columns // width, width)
    right_part = piece.reshape(every_amino_line, columns // width, width)
    outer = jnp.einsum("isc,jse->ijce", left_part, right_part, preferred_element_type=jnp.float32)
    outer = outer.astype(jnp.bfloat16).reshape(res_here, every_amino_line, width * width)
    update = (
        jnp.einsum("ijk,kz->ijz", outer, tensor_reduce_matrix, preferred_element_type=jnp.float32)
        / count[..., None]
    )
    resf = amino_presence.astype(jnp.float32)
    res_local = lax.dynamic_slice_in_dim(resf, res_start, res_here)
    pair_mask = res_local[:, None] * resf[None, :]
    couple_refreshed = (z_in + pair_mask[..., None] * update).astype(jnp.bfloat16)
    return (alignment_mixed, couple_refreshed)


def solution(mesh):
    in_specs = (
        P(("cplx", "dap"), None, None),
        P(("cplx", "dap"), None, None),
        P("cplx", None),
        P("cplx"),
        P("cplx"),
        P(),
        P(),
        P(),
        P(),
        P(),
        P(),
    )
    out_specs = (P(("cplx", "dap"), None, None), P(("cplx", "dap"), None, None))
    return jax.shard_map(
        on_device, mesh=mesh, in_specs=in_specs, out_specs=out_specs, check_vma=False
    )
```

profile of v0, /device:TPU:0, one launch (start us, length us, event | category | flops | bytes accessed | tf_op | source)
XLA Modules:
  0.0 88.1 jit_solution(13455693065240458379)
XLA Ops:
  0.6 0.0 copy-start
  0.6 0.0 copy-start.1
  0.7 0.8 dynamic_slice.12
  1.4 0.7 broadcast_subtract_fusion
  2.2 0.7 compare_convert_fusion
  2.9 0.9 %convert_reduce_fusion = f32[2,64]{1,0:T(2,128)S(1)} fusion(bf16[2,64,256]{2,1,0:T(8,128)(2,1)} %param.11), kind=kLoop, calls=%fused_computation.35 | loop fusion | flops 65408 | bytes 66048 | tf_op jit(solution)/shard_map/reduce_sum | solution.py:11
  3.8 1.0 %fusion.24 = f32[2,64]{1,0:T(2,128)S(1)} fusion(bf16[2,64,256]{2,1,0:T(8,128)(2,1)} %param.11, f32[2,64]{1,0:T(2,128)S(1)} %broadcast_multiply_fusion.3), kind=kLoop, calls=%fused_computation.42 | loop fusion | flops 130944 | bytes 66560 | tf_op jit(solution)/shard_map/reduce_sum | solution.py:12
  4.9 0.8 slice_bitcast_fusion.5
  5.6 1.2 %fusion.19 = f32[8,64]{1,0:T(8,128)S(1)} fusion(bf16[8,64,128]{2,1,0:T(8,128)(2,1)} %param.12, f32[128]{0:T(128)S(1)} %get-tuple-element.7, f32[8,64]{1,0:T(8,128)S(1)} %compare_convert_fusion, f32[128]{0:T(128)S(1)} %get-tuple-element.6, f32[8,64]{1,0:T(8,128)S(1)} %broadcast_subtract_fusion), kind=kLoop, calls=%fused_computation.33 | loop fusion | flops 392704 | bytes 138240 | tf_op jit(solution)/shard_map/reduce_sum | solution.py:11
  6.9 1.3 %multiply_reduce_fusion = f32[8,64]{1,0:T(8,128)S(1)} fusion(bf16[8,64,128]{2,1,0:T(8,128)(2,1)} %param.12, f32[8,64]{1,0:T(8,128)S(1)} %broadcast_multiply_fusion.1, f32[128]{0:T(128)S(1)} %get-tuple-element.7, f32[8,64]{1,0:T(8,128)S(1)} %compare_convert_fusion, f32[128]{0:T(128)S(1)} %get-tuple-element.6, f32[8,64]{1,0:T(8,128)S(1)} %broadcast_subtract_fusion), kind=kLoop, calls=%fused_computation.30 | loop fusion | flops 523776 | bytes 140288 | tf_op jit(solution)/shard_map/reduce_sum | solution.py:12
  8.2 0.7 convert_element_type.94
  8.9 1.4 %fusion.10 = bf16[8,8,64]{2,0,1:T(8,128)(2,1)S(1)} fusion(bf16[8,64,128]{2,1,0:T(8,128)(2,1)} %param.12, f32[8,64]{1,0:T(8,128)S(1)} %add_rsqrt_fusion, f32[8,64]{1,0:T(8,128)S(1)} %broadcast_multiply_fusion.1, f32[128]{0:T(128)S(1)} %get-tuple-element.7, f32[8,64]{1,0:T(8,128)S(1)} %compare_convert_fusion, f32[128]{0:T(128)S(1)} %get-tuple-element.6, ...), kind=kOutput, calls=%fused_computation.17 | convolution fusion | flops 1576960 | bytes 150528 | tf_op jit(solution)/shard_map/ijc,ch->hij/dot_general | solution.py:46
  10.2 32.3 %all_gather.6 = bf16[8,64,64]{2,0,1:T(8,128)(2,1)S(1)} all-gather(bf16[8,8,64]{2,0,1:T(8,128)(2,1)S(1)} %fusion.10), channel_id=1, replica_groups=mesh['cplx'=4,'dap'=8] {'dap'}, dimensions={1}, use_global_device_ids=true | all-gather | bytes 73728 | tf_op jit(solution)/shard_map/all_gather | solution.py:49
  42.6 0.1 copy.28
  42.7 1.2 %copy.27 = bf16[256,1024]{0,1:T(8,128)(2,1)S(1)} copy(bf16[256,1024]{1,0:T(8,128)(2,1)} %param.17) | data formatting | bytes 1048576 | tf_op args[6]
  44.0 0.0 copy-done.1
  44.0 0.4 fusion.49
  44.4 0.3 fusion.3
  44.7 0.0 copy-start.4
  44.7 0.1 fusion.50
  44.8 0.0 copy-start.5
  44.8 0.0 copy-start.6
  44.9 0.2 fusion.7
  45.1 0.5 copy-done.4
  45.6 0.3 convert_reduce_fusion.1
  45.9 0.0 copy-start.3
  45.9 0.2 fusion.26
  46.1 0.0 copy-done.5
  46.1 0.2 convolution_bitcast_fusion.1
  46.3 0.1 copy.31
  46.4 0.1 all_to_all.12
  46.5 0.7 reshape.178
  47.2 5.5 %all-to-all-start = ((bf16[8,2,256]{2,1,0:T(2,128)(2,1)}), bf16[8,2,256]{2,1,0:T(2,128)(2,1)S(1)}, u32[]{:S(2)}, u32[]{:S(2)}) async-start(bf16[8,2,256]{2,1,0:T(2,128)(2,1)} %reshape.178), calls=%async_computation | async-start | bytes 16384 | tf_op jit(solution)/shard_map/all_to_all | solution.py:105
  52.7 0.3 convolution_add_fusion.2
  53.0 0.0 copy-done.6
  53.0 0.1 dynamic_slice.14
  53.1 0.1 broadcast_multiply_fusion
  53.1 31.1 %all_gather.7 = bf16[64,512]{0,1:T(8,128)(2,1)S(1)} all-gather(bf16[64,64]{0,1:T(8,128)(2,1)S(1)} %bitcast.75), channel_id=1, replica_groups=mesh['cplx'=4,'dap'=8] {'dap'}, dimensions={1}, use_global_device_ids=true | all-gather | bytes 73728 | tf_op jit(solution)/shard_map/all_gather | solution.py:106
  84.2 0.0 all-to-all-done
  84.2 0.1 reshape.179
  84.3 0.1 reshape.175
  84.4 0.7 convert_bitcast_fusion
  85.1 0.0 copy-start.2
  85.1 1.4 %copy.34 = bf16[8,64,32,32]{1,3,2,0:T(8,128)(2,1)S(1)} copy(bf16[8,64,32,32]{1,2,0,3:T(8,128)(2,1)S(1)} %convert_bitcast_fusion) | data formatting | bytes 2097152 | tf_op jit(solution)/shard_map/convert_element_type | solution.py:111
  86.5 0.0 copy-done.3
  86.5 0.0 copy-done
  86.5 0.0 copy-done.2
  86.5 1.6 %fusion.8 = bf16[8,64,128]{2,1,0:T(8,128)(2,1)} fusion(bf16[8,64,1024]{1,2,0:T(8,128)(2,1)S(1)} %bitcast.72, bf16[1024,128]{1,0:T(8,128)(2,1)S(1)} %copy-done, bf16[8,64,128]{2,1,0:T(8,128)(2,1)S(1)} %copy-done.2, f32[8,64]{1,0:T(8,128)S(1)} %convolution_add_fusion.2, f32[8,64]{1,0:T(8,128)S(1)} %broadcast_multiply_fusion, f32[128]{0:T(128)S(1)} %get-tuple-element.7, ...), kind=kOutput, calls=%fused_computation.12 | convolution fusion | flops 134807552 | bytes 1582080 | tf_op jit(solution)/shard_map/ijk,kz->ijz/dot_general | solution.py:113
  (10 shorter events, 0.1 us)
Async XLA Ops:
  0.6 85.9 %copy-start = (bf16[1024,128]{1,0:T(8,128)(2,1)S(1)}, bf16[1024,128]{1,0:T(8,128)(2,1)}, u32[]{:S(2)}) copy-start(bf16[1024,128]{1,0:T(8,128)(2,1)} %param.21) | copy-start | bytes 786436
  0.6 43.3 %copy-start.1 = (bf16[2,64,256]{2,1,0:T(8,128)(2,1)S(1)}, bf16[2,64,256]{2,1,0:T(8,128)(2,1)}, u32[]{:S(2)}) copy-start(bf16[2,64,256]{2,1,0:T(8,128)(2,1)} %param.11) | copy-start | bytes 196612
  44.7 0.9 %copy-start.4 = (bf16[256,256]{1,0:T(8,128)(2,1)S(1)}, bf16[256,256]{1,0:T(8,128)(2,1)}, u32[]{:S(2)}) copy-start(bf16[256,256]{1,0:T(8,128)(2,1)} %param.18) | copy-start | bytes 393220
  44.8 1.2 %copy-start.5 = (bf16[256,64]{0,1:T(8,128)(2,1)S(1)}, bf16[256,64]{0,1:T(8,128)(2,1)}, u32[]{:S(2)}) copy-start(bf16[256,64]{0,1:T(8,128)(2,1)} %param.20) | copy-start | bytes 98308
  44.8 8.1 %copy-start.6 = (s32[64]{0:T(128)S(1)}, s32[64]{0:T(128)}, u32[]{:S(2)}) copy-start(s32[64]{0:T(128)} %param.14) | copy-start | bytes 772
  45.9 40.6 %copy-start.3 = (bf16[2,64,256]{2,1,0:T(8,128)(2,1)}, bf16[2,64,256]{2,1,0:T(8,128)(2,1)S(1)}, u32[]{:S(2)}) copy-start(bf16[2,64,256]{2,1,0:T(8,128)(2,1)S(1)} %get-tuple-element.11) | copy-start | bytes 196612
  47.2 37.0 %all-to-all-start = ((bf16[8,2,256]{2,1,0:T(2,128)(2,1)}), bf16[8,2,256]{2,1,0:T(2,128)(2,1)S(1)}, u32[]{:S(2)}, u32[]{:S(2)}) async-start(bf16[8,2,256]{2,1,0:T(2,128)(2,1)} %reshape.178), calls=%async_computation | async-start | bytes 16384 | tf_op jit(solution)/shard_map/all_to_all | solution.py:105
  85.1 1.4 %copy-start.2 = (bf16[8,64,128]{2,1,0:T(8,128)(2,1)S(1)}, bf16[8,64,128]{2,1,0:T(8,128)(2,1)}, u32[]{:S(2)}) copy-start(bf16[8,64,128]{2,1,0:T(8,128)(2,1)} %param.12) | copy-start | bytes 393220
where the time goes:
time: 88.6 us; the launch traced here: 88.1 us
  blocking collectives  63.4 us (72%)
  other arithmetic  7.06 us (8%)
  local copies, waits for them, and re-layouts  5.95 us (7%)
  starting transfers between devices  5.47 us (6%)
  matrix products  5.34 us (6%)
    all_gather x1, blocking collectives, on_device(): bias_all = lax.all_gather(bias_here, 'dap', axis=1, tiled=True)  32.3 us
    all_gather x1, blocking collectives, on_device(): piece = lax.all_gather(right_rows, 'dap', axis=1, tiled=True)  31.1 us
    all_to_all x1, starting transfers between devices, on_device(): lax.all_to_all(left_rows, 'dap', split_axis=0, concat_axis=1, tiled=True)  5.47 us
    unnamed x17, local copies, waits for them, and re-layouts  2.54 us
    reduce_sum x3, other arithmetic, standardize_features(): spread = jnp.mean(center * center, axis=-1, keepdims=True)  2.46 us
    reduce_sum x2, other arithmetic, standardize_features(): center = x - jnp.mean(x, axis=-1, keepdims=True)  2.16 us
  transfers between devices with their start and end apart: 1, of which 0 were waited for; matrix products, arithmetic and copies ran while one was open for 0% of the time, Pallas kernels for 0%

commit v1 on v0

--- a/solution.py
+++ b/solution.py
@@ -1,9 +1,25 @@
+import functools
 import jax
 import jax.numpy as jnp
 from jax import lax
 from jax.sharding import PartitionSpec as P
 
 EPS = 1e-05
+
+
+def raise_map(x_local, mesh_dim):
+    return jnp.concatenate(
+        jax.lax.all_to_all(
+            jnp.stack(jnp.split(x_local, jax.lax.axis_size(mesh_dim), axis=0), axis=0),
+            mesh_dim,
+            0,
+            0,
+        ),
+        axis=1,
+    )
+
+
+mix_leaf_over_axis = functools.partial(raise_map, mesh_dim="dap")
 
 
 def standardize_features(x):
@@ -102,7 +118,7 @@
         .astype(jnp.bfloat16)
         .reshape(every_amino_line, device_aligned_lines * width)
     )
-    left_full = lax.all_to_all(left_rows, "dap", split_axis=0, concat_axis=1, tiled=True)
+    left_full = mix_leaf_over_axis(left_rows)
     piece = lax.all_gather(right_rows, "dap", axis=1, tiled=True)
     columns = piece.shape[1]
     left_part = left_full.reshape(res_here, columns // width, width)

time: 88.6 us -> 89.2 us (level)
    unnamed x17 -> x24, local copies, waits for them, and re-layouts: 2.54 us -> 2.6 us
where the time goes in v1:
time: 89.2 us; the launch traced here: 88.7 us
  blocking collectives  63.4 us (71%)
  other arithmetic  7.06 us (8%)
  local copies, waits for them, and re-layouts  6.56 us (7%)
  starting transfers between devices  5.47 us (6%)
  matrix products  5.34 us (6%)
  between operations  0.9 us (1%)
    all_gather x1, blocking collectives, on_device(): bias_all = lax.all_gather(bias_here, 'dap', axis=1, tiled=True)  32.3 us
    all_gather x1, blocking collectives, on_device(): piece = lax.all_gather(right_rows, 'dap', axis=1, tiled=True)  31.1 us
    all_to_all x1, starting transfers between devices, raise_map(): jax.lax.all_to_all(jnp.stack(jnp.split(x_local, jax.lax.axis_size(mesh_di...  5.47 us
    unnamed x24, local copies, waits for them, and re-layouts  2.6 us
    reduce_sum x3, other arithmetic, standardize_features(): spread = jnp.mean(center * center, axis=-1, keepdims=True)  2.46 us
    reduce_sum x2, other arithmetic, standardize_features(): center = x - jnp.mean(x, axis=-1, keepdims=True)  2.16 us
  transfers between devices with their start and end apart: 1, of which 0 were waited for; matrix products, arithmetic and copies ran while one was open for 0% of the time, Pallas kernels for 0%

profile of v1, /device:TPU:0, one launch (start us, length us, event | category | flops | bytes accessed | tf_op | source)
XLA Modules:
  0.0 88.7 jit_solution(8231396437722377889)
XLA Ops:
  0.6 0.0 copy-start
  0.6 0.0 copy-start.1
  0.7 0.8 dynamic_slice.12
  1.4 0.7 broadcast_subtract_fusion
  2.2 0.7 compare_convert_fusion
  2.9 0.9 %convert_reduce_fusion = f32[2,64]{1,0:T(2,128)S(1)} fusion(bf16[2,64,256]{2,1,0:T(8,128)(2,1)} %param.11), kind=kLoop, calls=%fused_computation.35 | loop fusion | flops 65408 | bytes 66048 | tf_op jit(solution)/shard_map/reduce_sum | solution.py:27
  3.8 1.0 %fusion.24 = f32[2,64]{1,0:T(2,128)S(1)} fusion(bf16[2,64,256]{2,1,0:T(8,128)(2,1)} %param.11, f32[2,64]{1,0:T(2,128)S(1)} %broadcast_multiply_fusion.3), kind=kLoop, calls=%fused_computation.42 | loop fusion | flops 130944 | bytes 66560 | tf_op jit(solution)/shard_map/reduce_sum | solution.py:28
  4.9 0.8 slice_bitcast_fusion.5
  5.6 1.2 %fusion.19 = f32[8,64]{1,0:T(8,128)S(1)} fusion(bf16[8,64,128]{2,1,0:T(8,128)(2,1)} %param.12, f32[128]{0:T(128)S(1)} %get-tuple-element.15, f32[8,64]{1,0:T(8,128)S(1)} %compare_convert_fusion, f32[128]{0:T(128)S(1)} %get-tuple-element.14, f32[8,64]{1,0:T(8,128)S(1)} %broadcast_subtract_fusion), kind=kLoop, calls=%fused_computation.33 | loop fusion | flops 392704 | bytes 138240 | tf_op jit(solution)/shard_map/reduce_sum | solution.py:27
  6.9 1.3 %multiply_reduce_fusion = f32[8,64]{1,0:T(8,128)S(1)} fusion(bf16[8,64,128]{2,1,0:T(8,128)(2,1)} %param.12, f32[8,64]{1,0:T(8,128)S(1)} %broadcast_multiply_fusion.1, f32[128]{0:T(128)S(1)} %get-tuple-element.15, f32[8,64]{1,0:T(8,128)S(1)} %compare_convert_fusion, f32[128]{0:T(128)S(1)} %get-tuple-element.14, f32[8,64]{1,0:T(8,128)S(1)} %broadcast_subtract_fusion), kind=kLoop, calls=%fused_computation.30 | loop fusion | flops 523776 | bytes 140288 | tf_op jit(solution)/shard_map/reduce_sum | solution.py:28
  8.2 0.7 convert_element_type.94
  8.9 1.4 %fusion.10 = bf16[8,8,64]{2,0,1:T(8,128)(2,1)S(1)} fusion(bf16[8,64,128]{2,1,0:T(8,128)(2,1)} %param.12, f32[8,64]{1,0:T(8,128)S(1)} %add_rsqrt_fusion, f32[8,64]{1,0:T(8,128)S(1)} %broadcast_multiply_fusion.1, f32[128]{0:T(128)S(1)} %get-tuple-element.15, f32[8,64]{1,0:T(8,128)S(1)} %compare_convert_fusion, f32[128]{0:T(128)S(1)} %get-tuple-element.14, ...), kind=kOutput, calls=%fused_computation.17 | convolution fusion | flops 1576960 | bytes 150528 | tf_op jit(solution)/shard_map/ijc,ch->hij/dot_general | solution.py:62
  10.2 32.3 %all_gather.6 = bf16[8,64,64]{2,0,1:T(8,128)(2,1)S(1)} all-gather(bf16[8,8,64]{2,0,1:T(8,128)(2,1)S(1)} %fusion.10), channel_id=1, replica_groups=mesh['cplx'=4,'dap'=8] {'dap'}, dimensions={1}, use_global_device_ids=true | all-gather | bytes 73728 | tf_op jit(solution)/shard_map/all_gather | solution.py:65
  42.6 0.1 copy.27
  42.7 1.2 %copy.26 = bf16[256,1024]{0,1:T(8,128)(2,1)S(1)} copy(bf16[256,1024]{1,0:T(8,128)(2,1)} %param.17) | data formatting | bytes 1048576 | tf_op args[6]
  44.0 0.4 fusion.50
  44.4 0.3 fusion.3
  44.7 0.0 copy-start.4
  44.7 0.1 fusion.51
  44.8 0.0 copy-start.5
  44.8 0.0 copy-start.6
  44.9 0.2 fusion.7
  45.1 0.5 copy-done.4
  45.6 0.3 convert_reduce_fusion.1
  45.9 0.2 fusion.26
  46.1 0.2 convolution_bitcast_fusion.1
  46.3 0.1 fusion.49
  46.4 0.1 copy.37
  46.5 0.1 copy.36
  46.6 0.1 copy.35
  46.7 0.1 copy.34
  46.8 0.1 copy.33
  46.8 0.1 copy.32
  46.9 0.1 copy.31
  47.0 0.1 copy.30
  47.2 0.7 reshape.189
  47.9 5.5 %all-to-all-start = ((bf16[8,2,256]{2,1,0:T(2,128)(2,1)}), bf16[8,2,256]{2,1,0:T(2,128)(2,1)S(1)}, u32[]{:S(2)}, u32[]{:S(2)}) async-start(bf16[8,2,256]{2,1,0:T(2,128)(2,1)} %reshape.189), calls=%async_computation | async-start | bytes 16384 | tf_op jit(solution)/shard_map/all_to_all | solution.py:12
  53.3 0.3 convolution_add_fusion.2
  53.6 0.1 dynamic_slice.14
  53.7 0.1 broadcast_multiply_fusion
  53.8 31.1 %all_gather.7 = bf16[64,512]{0,1:T(8,128)(2,1)S(1)} all-gather(bf16[64,64]{0,1:T(8,128)(2,1)S(1)} %bitcast.83), channel_id=1, replica_groups=mesh['cplx'=4,'dap'=8] {'dap'}, dimensions={1}, use_global_device_ids=true | all-gather | bytes 73728 | tf_op jit(solution)/shard_map/all_gather | solution.py:122
  84.8 0.0 all-to-all-done
  84.8 0.1 reshape.190
  84.9 0.1 reshape.186
  85.0 0.7 convert_bitcast_fusion
  85.8 0.0 copy-start.2
  85.8 1.4 %copy.40 = bf16[8,64,32,32]{1,3,2,0:T(8,128)(2,1)S(1)} copy(bf16[8,64,32,32]{1,2,0,3:T(8,128)(2,1)S(1)} %convert_bitcast_fusion) | data formatting | bytes 2097152 | tf_op jit(solution)/shard_map/convert_element_type | solution.py:127
  87.2 1.6 %fusion.8 = bf16[8,64,128]{2,1,0:T(8,128)(2,1)} fusion(bf16[8,64,1024]{1,2,0:T(8,128)(2,1)S(1)} %bitcast.80, bf16[1024,128]{1,0:T(8,128)(2,1)S(1)} %copy-done, bf16[8,64,128]{2,1,0:T(8,128)(2,1)S(1)} %copy-done.2, f32[8,64]{1,0:T(8,128)S(1)} %convolution_add_fusion.2, f32[8,64]{1,0:T(8,128)S(1)} %broadcast_multiply_fusion, f32[128]{0:T(128)S(1)} %get-tuple-element.15, ...), kind=kOutput, calls=%fused_computation.12 | convolution fusion | flops 134807552 | bytes 1582080 | tf_op jit(solution)/shard_map/ijk,kz->ijz/dot_general | solution.py:129
  (25 shorter events, 0.2 us)
Async XLA Ops:
  0.6 86.5 %copy-start = (bf16[1024,128]{1,0:T(8,128)(2,1)S(1)}, bf16[1024,128]{1,0:T(8,128)(2,1)}, u32[]{:S(2)}) copy-start(bf16[1024,128]{1,0:T(8,128)(2,1)} %param.21) | copy-start | bytes 786436
  0.6 43.3 %copy-start.1 = (bf16[2,64,256]{2,1,0:T(8,128)(2,1)S(1)}, bf16[2,64,256]{2,1,0:T(8,128)(2,1)}, u32[]{:S(2)}) copy-start(bf16[2,64,256]{2,1,0:T(8,128)(2,1)} %param.11) | copy-start | bytes 196612
  44.7 0.9 %copy-start.4 = (bf16[256,256]{1,0:T(8,128)(2,1)S(1)}, bf16[256,256]{1,0:T(8,128)(2,1)}, u32[]{:S(2)}) copy-start(bf16[256,256]{1,0:T(8,128)(2,1)} %param.18) | copy-start | bytes 393220
  44.8 1.2 %copy-start.5 = (bf16[256,64]{0,1:T(8,128)(2,1)S(1)}, bf16[256,64]{0,1:T(8,128)(2,1)}, u32[]{:S(2)}) copy-start(bf16[256,64]{0,1:T(8,128)(2,1)} %param.20) | copy-start | bytes 98308
  44.8 8.8 %copy-start.6 = (s32[64]{0:T(128)S(1)}, s32[64]{0:T(128)}, u32[]{:S(2)}) copy-start(s32[64]{0:T(128)} %param.14) | copy-start | bytes 772
  45.9 41.3 %copy-start.3 = (bf16[2,64,256]{2,1,0:T(8,128)(2,1)}, bf16[2,64,256]{2,1,0:T(8,128)(2,1)S(1)}, u32[]{:S(2)}) copy-start(bf16[2,64,256]{2,1,0:T(8,128)(2,1)S(1)} %get-tuple-element.19) | copy-start | bytes 196612
  47.9 37.0 %all-to-all-start = ((bf16[8,2,256]{2,1,0:T(2,128)(2,1)}), bf16[8,2,256]{2,1,0:T(2,128)(2,1)S(1)}, u32[]{:S(2)}, u32[]{:S(2)}) async-start(bf16[8,2,256]{2,1,0:T(2,128)(2,1)} %reshape.189), calls=%async_computation | async-start | bytes 16384 | tf_op jit(solution)/shard_map/all_to_all | solution.py:12
  85.8 1.4 %copy-start.2 = (bf16[8,64,128]{2,1,0:T(8,128)(2,1)S(1)}, bf16[8,64,128]{2,1,0:T(8,128)(2,1)}, u32[]{:S(2)}) copy-start(bf16[8,64,128]{2,1,0:T(8,128)(2,1)} %param.12) | copy-start | bytes 393220
